TPU v7x, 256 devices: a whole 4x4x8 slice. The times are simulated.
256 devices in a mesh: mem: 32 (over y, x, core), col: 8 (over z).
Axes of the slice: x: 4, y: 4, z: 8, core: 2. Of those that a mesh axis runs over, the one named last changes fastest.
Arguments:
- background_trials: bfloat16 [256, 4, 128, 1024], P('mem', None, None, 'col'), may hold values from -6 to 6
- region_active_tally: int32 [32, 32], P('mem', 'col'), may hold values from 256 to 2048, as said below
- sensed_component: int32 [32, 32, 2048], P('mem', 'col'), may hold values from 0 to 1919
- distance_bucket: int32 [32, 32, 2048], P('mem', 'col'), may hold values from 0 to 15
- sensor_readings: float32 [32, 32, 2048], P('mem', 'col'), may hold values from -6 to 6
- inverse_noise_variance: float32 [32, 32, 2048], P('mem', 'col'), may hold values from 0.25 to 4
- localization_factors: float32 [16], replicated, may hold values from 0.05 to 1
Outputs:
- analysis: bfloat16 [256, 4, 128, 1024], P('mem', None, None, 'col')
Inputs may be any that keep to these rules, and one draw needn't show every extreme that they name: `region_active_tally`: observations of a patch fill its first slots; some patch has exactly 2048 live observations.
All inputs are finite; a program needn't handle non-finite values.
Results may differ from a plain program's by a relative error of at most 0.0063.
Values may be sent and summed in bfloat16 or wider, within the bound.
A program may use at most 64 MiB of HBM per device.

v0:
```python
import jax
import jax.numpy as jnp
from jax import lax
from jax.sharding import PartitionSpec as P

SECTOR_SPAN = 32
REACH_MARGIN = 4
ITERS = 4


inflation = 1.1
obs_block = 128


def padded(block, sides, width):
    for axis, dim in sides:
        count = lax.axis_size(axis)
        forward = [(i, i + 1) for i in range(count - 1)]
        backward = [(target, source) for source, target in forward]
        low = lax.ppermute(
            lax.slice_in_dim(block, block.shape[dim] - width, None, axis=dim), axis, forward
        )
        high = lax.ppermute(lax.slice_in_dim(block, 0, width, axis=dim), axis, backward)
        block = jnp.concatenate([low, block, high], axis=dim)
    return block


def lookup(class_ids, weight_table):
    table_slots = jnp.arange(weight_table.shape[0], dtype=jnp.int32)
    return jnp.sum(jnp.where(class_ids[..., None] == table_slots, weight_table, 0.0), axis=-1)


def observe(
    anomaly_flat, average_flat, cell_ids, class_ids, values, inv_var, is_live, weight_table
):
    observed = jnp.take_along_axis(anomaly_flat, cell_ids[:, None, :], axis=2)
    innovation = values - jnp.take_along_axis(average_flat, cell_ids, axis=1)
    weight = jnp.where(is_live, inv_var * lookup(class_ids, weight_table), 0.0)
    scaled = (observed.astype(jnp.float32) * weight[:, None, :]).astype(jnp.bfloat16)
    gram_part = jnp.einsum("qkm,qjm->qkj", scaled, observed, preferred_element_type=jnp.float32)
    forcing_part = jnp.einsum(
        "qkm,qm->qk", scaled.astype(jnp.float32), innovation, precision=lax.Precision.HIGHEST
    )
    return (gram_part, forcing_part)


def local(
    background_trials,
    region_active_tally,
    sensed_component,
    distance_bucket,
    sensor_readings,
    inverse_noise_variance,
    localization_factors,
):
    local_region_tile = lax.all_to_all(
        background_trials, "mem", split_axis=2, concat_axis=0, tiled=True
    )
    enlarged_piece = padded(local_region_tile, (("mem", 2), ("col", 3)), REACH_MARGIN)
    trial_flattened = enlarged_piece.shape[0]
    physical_quantity_stack = enlarged_piece.shape[1]
    tile_height = enlarged_piece.shape[2] - 2 * REACH_MARGIN
    tile_width = enlarged_piece.shape[3] - 2 * REACH_MARGIN
    patches = tile_width // SECTOR_SPAN
    frame_breadth = SECTOR_SPAN + 2 * REACH_MARGIN
    unit_weights = jnp.ones((trial_flattened,), jnp.bfloat16)
    predicted_average = (
        lax.dot_general(
            unit_weights,
            enlarged_piece,
            (((0,), (0,)), ((), ())),
            preferred_element_type=jnp.float32,
        )
        / trial_flattened
    )
    deviation_matrix = (enlarged_piece.astype(jnp.float32) - predicted_average).astype(jnp.bfloat16)
    anomaly_flat = jnp.stack(
        [
            deviation_matrix[
                :, :, :, sector_index * SECTOR_SPAN : sector_index * SECTOR_SPAN + frame_breadth
            ]
            for sector_index in range(patches)
        ]
    ).reshape(patches, trial_flattened, -1)
    average_flat = jnp.stack(
        [
            predicted_average[
                :, :, sector_index * SECTOR_SPAN : sector_index * SECTOR_SPAN + frame_breadth
            ]
            for sector_index in range(patches)
        ]
    ).reshape(patches, -1)
    counts = region_active_tally.reshape(patches)
    cell_ids = sensed_component.reshape(patches, -1)
    class_ids = distance_bucket.reshape(patches, -1)
    values = sensor_readings.reshape(patches, -1)
    inv_vars = inverse_noise_variance.reshape(patches, -1)
    order_ids = jnp.broadcast_to(jnp.arange(cell_ids.shape[1], dtype=jnp.int32), cell_ids.shape)
    rounds = (jnp.max(counts) + obs_block - 1) // obs_block

    def one_round(round_id, partial_sums):
        block_start = round_id * obs_block

        def take_block(source):
            return lax.dynamic_slice_in_dim(source, block_start, obs_block, 1)

        gram_part, forcing_part = observe(
            anomaly_flat,
            average_flat,
            take_block(cell_ids),
            take_block(class_ids),
            take_block(values),
            take_block(inv_vars),
            take_block(order_ids) < counts[:, None],
            localization_factors,
        )
        return (partial_sums[0] + gram_part, partial_sums[1] + forcing_part)

    initial = (
        jnp.zeros((patches, trial_flattened, trial_flattened), jnp.float32),
        jnp.zeros((patches, trial_flattened), jnp.float32),
    )
    gram_sum, forcing = lax.fori_loop(0, rounds, one_round, initial)
    identity = jnp.eye(trial_flattened, dtype=jnp.float32)
    gram_sum = gram_sum + (trial_flattened - 1) / inflation * identity
    norm_scale = jnp.sqrt(jnp.sum(gram_sum * gram_sum, axis=(1, 2)))
    iterate = gram_sum / norm_scale[:, None, None]
    inverse_root = jnp.broadcast_to(identity, iterate.shape)
    for sweep_id in range(ITERS):
        factor = 1.5 * identity - 0.5 * jnp.einsum(
            "qij,qjk->qik", inverse_root, iterate, precision=lax.Precision.HIGHEST
        )
        if sweep_id + 1 < ITERS:
            iterate = jnp.einsum("qij,qjk->qik", iterate, factor, precision=lax.Precision.HIGHEST)
        inverse_root = jnp.einsum(
            "qij,qjk->qik", factor, inverse_root, precision=lax.Precision.HIGHEST
        )
    partial_shift = jnp.einsum("qij,qj->qi", inverse_root, forcing, precision=lax.Precision.HIGHEST)
    mean_shift = (
        jnp.einsum("qij,qj->qi", inverse_root, partial_shift, precision=lax.Precision.HIGHEST)
        / norm_scale[:, None]
    )
    spread_scale = jnp.sqrt((trial_flattened - 1.0) / norm_scale)
    transform = (spread_scale[:, None, None] * inverse_root + mean_shift[:, :, None]).astype(
        jnp.bfloat16
    )
    own_anomaly = deviation_matrix[
        :, :, REACH_MARGIN : REACH_MARGIN + tile_height, REACH_MARGIN : REACH_MARGIN + tile_width
    ].reshape(trial_flattened, physical_quantity_stack, tile_height, patches, SECTOR_SPAN)
    inner_midpoint = predicted_average[
        :, REACH_MARGIN : REACH_MARGIN + tile_height, REACH_MARGIN : REACH_MARGIN + tile_width
    ].reshape(physical_quantity_stack, tile_height, patches, SECTOR_SPAN)
    analysed = (
        jnp.einsum("kstqp,qkj->jstqp", own_anomaly, transform, preferred_element_type=jnp.float32)
        + inner_midpoint[None]
    )
    analysed = analysed.astype(jnp.bfloat16).reshape(
        trial_flattened, physical_quantity_stack, tile_height, tile_width
    )
    return lax.all_to_all(analysed, "mem", split_axis=0, concat_axis=2, tiled=True)


def solution(mesh):
    placed = (
        P("mem", None, None, "col"),
        P("mem", "col"),
        P("mem", "col", None),
        P("mem", "col", None),
        P("mem", "col", None),
        P("mem", "col", None),
        P(),
    )
    return jax.shard_map(
        local, mesh=mesh, in_specs=placed, out_specs=P("mem", None, None, "col"), check_vma=False
    )
```

profile of v0, /device:TPU:1, one launch (start us, length us, event | category | flops | bytes accessed | tf_op | source)
XLA Modules:
  0.0 392.2 jit_solution(2368583581429825270)
XLA Ops:
  1.9 25.6 %all_to_all.36 = bf16[8,4,128,128]{3,0,1,2:T(8,128)(2,1)S(1)} all-to-all(bf16[8,4,128,128]{3,0,1,2:T(8,128)(2,1)S(1)} %copy.56), channel_id=1, replica_groups=mesh['mem'=32,'col'=8] {'mem'}, dimensions={2} | all-to-all | bytes 2097152 | tf_op jit(solution)/shard_map/all_to_all | solution.py:56
  34.2 7.7 %collective-permute-done = bf16[256,4,4,128]{3,0,2,1:T(8,128)(2,1)S(1)} collective-permute-done((bf16[256,4,4,128]{3,0,2,1:T(8,128)(2,1)S(1)}, bf16[256,4,4,128]{3,0,2,1:T(8,128)(2,1)S(1)}, u32[]{:S(2)}, u32[]{:S(2)}) %collective-permute-start) | collective-permute-done | bytes 1048608 | tf_op jit(solution)/shard_map/ppermute | solution.py:20
  42.0 4.4 %collective-permute-done.1 = bf16[256,4,4,128]{3,0,2,1:T(8,128)(2,1)S(1)} collective-permute-done((bf16[256,4,4,128]{3,0,2,1:T(8,128)(2,1)S(1)}, bf16[256,4,4,128]{3,0,2,1:T(8,128)(2,1)S(1)}, u32[]{:S(2)}, u32[]{:S(2)}) %collective-permute-start.1) | collective-permute-done | bytes 1048608 | tf_op jit(solution)/shard_map/ppermute | solution.py:23
  47.7 3.0 fusion.34
  50.7 3.2 copy.59
  54.0 4.2 %collective-permute-start.2 = (bf16[256,4,12,4]{0,3,2,1:T(4,128)(2,1)S(1)}, bf16[256,4,12,4]{0,3,2,1:T(4,128)(2,1)}, u32[]{:S(2)}, u32[]{:S(2)}) collective-permute-start(bf16[256,4,12,4]{0,3,2,1:T(4,128)(2,1)S(1)} %copy.59), channel_id=1, source_target_pairs={{0,1},{1,2},{2,3},{3,4},{4,5},{5,6},{6,7},{8,9},{9,10},{10,11},{11... | collective-permute-start | bytes 294920 | tf_op jit(solution)/shard_map/ppermute | solution.py:20
  66.0 3.6 copy.62
  69.5 7.1 %fusion.29 = f32[1,4,12,136]{3,0,2,1:T(1,128)S(1)} fusion(bf16[256,4,12,4]{3,0,2,1:T(8,128)(2,1)} %copy.62, bf16[256,4,4,128]{3,0,2,1:T(8,128)(2,1)} %copy-done.3, bf16[256,4,4,128]{3,0,2,1:T(8,128)(2,1)} %bitcast.99, bf16[256,4,4,128]{3,0,2,1:T(8,128)(2,1)} %copy-done.2, bf16[256,4,12,4]{3,0,2,1:T(8,128)(2,1)S(1)} %copy.61), kind=kOutput, calls=%fused_computation.62 | convolution fusion | flops 20054016 | bytes 3368448 | tf_op jit(solution)/shard_map/dot_general | solution.py:68
  79.8 8.0 %subtract_convert_fusion = bf16[256,4,12,136]{3,0,2,1:T(8,128)(2,1)S(1)} fusion(f32[4,12,136]{2,1,0:T(8,128)S(1)} %bitcast_multiply_fusion, bf16[256,4,12,4]{3,0,2,1:T(8,128)(2,1)} %copy.62, bf16[256,4,4,128]{3,0,2,1:T(8,128)(2,1)} %copy-done.3, bf16[256,4,4,128]{3,0,2,1:T(8,128)(2,1)} %bitcast.100, bf16[256,4,4,128]{3,0,2,1:T(8,128)(2,1)} %copy-done.2, ...), kind=kLoop, calls=%fused_computation.24 | loop fusion | flops 20054016 | bytes 6710784 | tf_op jit(solution)/shard_map/convert_element_type | solution.py:76
  87.9 5.4 %fusion.33 = (bf16[256,4,12,40]{3,0,2,1:T(8,128)(2,1)}, bf16[256,4,12,40]{3,0,2,1:T(8,128)(2,1)S(1)}, bf16[256,4,12,40]{3,0,2,1:T(8,128)(2,1)}, bf16[256,4,12,40]{3,0,2,1:T(8,128)(2,1)}) fusion(bf16[256,4,12,136]{3,0,2,1:T(8,128)(2,1)S(1)} %subtract_convert_fusion), kind=kLoop, calls=%fused_computation.67 | loop fusion | bytes 7864320 | tf_op jit(solution)/shard_map/slice | solution.py:79
  93.3 4.1 %copy.63 = bf16[256,4,12,40]{0,3,2,1:T(8,128)(2,1)} copy(bf16[256,4,12,40]{3,0,2,1:T(8,128)(2,1)} %get-tuple-element.105) | data formatting | bytes 1966080 | tf_op jit(solution)/shard_map/slice | solution.py:79
  97.3 4.1 %copy.64 = bf16[256,4,12,40]{0,3,2,1:T(8,128)(2,1)} copy(bf16[256,4,12,40]{3,0,2,1:T(8,128)(2,1)} %get-tuple-element.108) | data formatting | bytes 1966080 | tf_op jit(solution)/shard_map/slice | solution.py:79
  101.4 4.1 %copy.65 = bf16[256,4,12,40]{0,3,2,1:T(8,128)(2,1)} copy(bf16[256,4,12,40]{3,0,2,1:T(8,128)(2,1)} %get-tuple-element.107) | data formatting | bytes 1966080 | tf_op jit(solution)/shard_map/slice | solution.py:79
  107.8 3.7 pad_maximum_fusion.1
  111.6 234.2 %while.12 = (s32[]{:T(128)}, f32[4,256,256]{2,1,0:T(8,128)S(1)}, f32[4,256]{1,0:T(4,128)S(1)}, s32[]{:T(128)}, s32[4,2048]{1,0:T(4,128)}, /*index=5*/bf16[4,256,...) while((s32[]{:T(128)}, f32[4,256,256]{2,1,0:T(8,128)S(1)}, ...), condition=%wide.region_3.4_spmd, body=%wide.region_1.3_spmd.sunk | while | flops 70158344 | bytes 3735335 | solution.py:123
  112.4 4.8 %gather_fusion = f32[512]{0:T(512)S(1)} fusion(f32[4,1920]{1,0:T(4,128)S(1)} %get-tuple-element.251, s32[512]{0:T(512)S(1)} %fusion.67), kind=kCustom, calls=%fused_computation.1.clone.1 | custom fusion | bytes 8192 | tf_op jit(solution)/shard_map/while/body/jit(take_along_axis)/gather | solution.py:37
  118.8 6.6 %gather_fusion.1 = bf16[512,256]{1,0:T(8,128)(2,1)S(1)} fusion(bf16[4,256,1920]{1,2,0:T(8,128)(2,1)} %get-tuple-element.244, s32[512]{0:T(512)S(1)} %fusion.67), kind=kCustom, calls=%fused_computation.clone.1 | custom fusion | bytes 528384 | tf_op jit(solution)/shard_map/while/body/jit(take_along_axis)/gather | solution.py:36
  127.0 4.8 %gather_fusion = f32[512]{0:T(512)S(1)} fusion(f32[4,1920]{1,0:T(4,128)S(1)} %get-tuple-element.251, s32[512]{0:T(512)S(1)} %fusion.67), kind=kCustom, calls=%fused_computation.1.clone.1 | custom fusion | bytes 8192 | tf_op jit(solution)/shard_map/while/body/jit(take_along_axis)/gather | solution.py:37
  133.4 6.6 %gather_fusion.1 = bf16[512,256]{1,0:T(8,128)(2,1)S(1)} fusion(bf16[4,256,1920]{1,2,0:T(8,128)(2,1)} %get-tuple-element.244, s32[512]{0:T(512)S(1)} %fusion.67), kind=kCustom, calls=%fused_computation.clone.1 | custom fusion | bytes 528384 | tf_op jit(solution)/shard_map/while/body/jit(take_along_axis)/gather | solution.py:36
  141.7 4.8 %gather_fusion = f32[512]{0:T(512)S(1)} fusion(f32[4,1920]{1,0:T(4,128)S(1)} %get-tuple-element.251, s32[512]{0:T(512)S(1)} %fusion.67), kind=kCustom, calls=%fused_computation.1.clone.1 | custom fusion | bytes 8192 | tf_op jit(solution)/shard_map/while/body/jit(take_along_axis)/gather | solution.py:37
  148.1 6.6 %gather_fusion.1 = bf16[512,256]{1,0:T(8,128)(2,1)S(1)} fusion(bf16[4,256,1920]{1,2,0:T(8,128)(2,1)} %get-tuple-element.244, s32[512]{0:T(512)S(1)} %fusion.67), kind=kCustom, calls=%fused_computation.clone.1 | custom fusion | bytes 528384 | tf_op jit(solution)/shard_map/while/body/jit(take_along_axis)/gather | solution.py:36
  156.3 4.8 %gather_fusion = f32[512]{0:T(512)S(1)} fusion(f32[4,1920]{1,0:T(4,128)S(1)} %get-tuple-element.251, s32[512]{0:T(512)S(1)} %fusion.67), kind=kCustom, calls=%fused_computation.1.clone.1 | custom fusion | bytes 8192 | tf_op jit(solution)/shard_map/while/body/jit(take_along_axis)/gather | solution.py:37
  162.7 6.6 %gather_fusion.1 = bf16[512,256]{1,0:T(8,128)(2,1)S(1)} fusion(bf16[4,256,1920]{1,2,0:T(8,128)(2,1)} %get-tuple-element.244, s32[512]{0:T(512)S(1)} %fusion.67), kind=kCustom, calls=%fused_computation.clone.1 | custom fusion | bytes 528384 | tf_op jit(solution)/shard_map/while/body/jit(take_along_axis)/gather | solution.py:36
  170.9 4.8 %gather_fusion = f32[512]{0:T(512)S(1)} fusion(f32[4,1920]{1,0:T(4,128)S(1)} %get-tuple-element.251, s32[512]{0:T(512)S(1)} %fusion.67), kind=kCustom, calls=%fused_computation.1.clone.1 | custom fusion | bytes 8192 | tf_op jit(solution)/shard_map/while/body/jit(take_along_axis)/gather | solution.py:37
  177.3 6.6 %gather_fusion.1 = bf16[512,256]{1,0:T(8,128)(2,1)S(1)} fusion(bf16[4,256,1920]{1,2,0:T(8,128)(2,1)} %get-tuple-element.244, s32[512]{0:T(512)S(1)} %fusion.67), kind=kCustom, calls=%fused_computation.clone.1 | custom fusion | bytes 528384 | tf_op jit(solution)/shard_map/while/body/jit(take_along_axis)/gather | solution.py:36
  185.5 4.8 %gather_fusion = f32[512]{0:T(512)S(1)} fusion(f32[4,1920]{1,0:T(4,128)S(1)} %get-tuple-element.251, s32[512]{0:T(512)S(1)} %fusion.67), kind=kCustom, calls=%fused_computation.1.clone.1 | custom fusion | bytes 8192 | tf_op jit(solution)/shard_map/while/body/jit(take_along_axis)/gather | solution.py:37
  191.9 6.6 %gather_fusion.1 = bf16[512,256]{1,0:T(8,128)(2,1)S(1)} fusion(bf16[4,256,1920]{1,2,0:T(8,128)(2,1)} %get-tuple-element.244, s32[512]{0:T(512)S(1)} %fusion.67), kind=kCustom, calls=%fused_computation.clone.1 | custom fusion | bytes 528384 | tf_op jit(solution)/shard_map/while/body/jit(take_along_axis)/gather | solution.py:36
  200.1 4.8 %gather_fusion = f32[512]{0:T(512)S(1)} fusion(f32[4,1920]{1,0:T(4,128)S(1)} %get-tuple-element.251, s32[512]{0:T(512)S(1)} %fusion.67), kind=kCustom, calls=%fused_computation.1.clone.1 | custom fusion | bytes 8192 | tf_op jit(solution)/shard_map/while/body/jit(take_along_axis)/gather | solution.py:37
  206.5 6.7 %gather_fusion.1 = bf16[512,256]{1,0:T(8,128)(2,1)S(1)} fusion(bf16[4,256,1920]{1,2,0:T(8,128)(2,1)} %get-tuple-element.244, s32[512]{0:T(512)S(1)} %fusion.67), kind=kCustom, calls=%fused_computation.clone.1 | custom fusion | bytes 528384 | tf_op jit(solution)/shard_map/while/body/jit(take_along_axis)/gather | solution.py:36
  214.8 4.8 %gather_fusion = f32[512]{0:T(512)S(1)} fusion(f32[4,1920]{1,0:T(4,128)S(1)} %get-tuple-element.251, s32[512]{0:T(512)S(1)} %fusion.67), kind=kCustom, calls=%fused_computation.1.clone.1 | custom fusion | bytes 8192 | tf_op jit(solution)/shard_map/while/body/jit(take_along_axis)/gather | solution.py:37
  221.2 6.6 %gather_fusion.1 = bf16[512,256]{1,0:T(8,128)(2,1)S(1)} fusion(bf16[4,256,1920]{1,2,0:T(8,128)(2,1)} %get-tuple-element.244, s32[512]{0:T(512)S(1)} %fusion.67), kind=kCustom, calls=%fused_computation.clone.1 | custom fusion | bytes 528384 | tf_op jit(solution)/shard_map/while/body/jit(take_along_axis)/gather | solution.py:36
  229.4 4.8 %gather_fusion = f32[512]{0:T(512)S(1)} fusion(f32[4,1920]{1,0:T(4,128)S(1)} %get-tuple-element.251, s32[512]{0:T(512)S(1)} %fusion.67), kind=kCustom, calls=%fused_computation.1.clone.1 | custom fusion | bytes 8192 | tf_op jit(solution)/shard_map/while/body/jit(take_along_axis)/gather | solution.py:37
  235.8 6.6 %gather_fusion.1 = bf16[512,256]{1,0:T(8,128)(2,1)S(1)} fusion(bf16[4,256,1920]{1,2,0:T(8,128)(2,1)} %get-tuple-element.244, s32[512]{0:T(512)S(1)} %fusion.67), kind=kCustom, calls=%fused_computation.clone.1 | custom fusion | bytes 528384 | tf_op jit(solution)/shard_map/while/body/jit(take_along_axis)/gather | solution.py:36
  244.0 4.8 %gather_fusion = f32[512]{0:T(512)S(1)} fusion(f32[4,1920]{1,0:T(4,128)S(1)} %get-tuple-element.251, s32[512]{0:T(512)S(1)} %fusion.67), kind=kCustom, calls=%fused_computation.1.clone.1 | custom fusion | bytes 8192 | tf_op jit(solution)/shard_map/while/body/jit(take_along_axis)/gather | solution.py:37
  250.4 6.6 %gather_fusion.1 = bf16[512,256]{1,0:T(8,128)(2,1)S(1)} fusion(bf16[4,256,1920]{1,2,0:T(8,128)(2,1)} %get-tuple-element.244, s32[512]{0:T(512)S(1)} %fusion.67), kind=kCustom, calls=%fused_computation.clone.1 | custom fusion | bytes 528384 | tf_op jit(solution)/shard_map/while/body/jit(take_along_axis)/gather | solution.py:36
  258.6 4.8 %gather_fusion = f32[512]{0:T(512)S(1)} fusion(f32[4,1920]{1,0:T(4,128)S(1)} %get-tuple-element.251, s32[512]{0:T(512)S(1)} %fusion.67), kind=kCustom, calls=%fused_computation.1.clone.1 | custom fusion | bytes 8192 | tf_op jit(solution)/shard_map/while/body/jit(take_along_axis)/gather | solution.py:37
  265.0 6.6 %gather_fusion.1 = bf16[512,256]{1,0:T(8,128)(2,1)S(1)} fusion(bf16[4,256,1920]{1,2,0:T(8,128)(2,1)} %get-tuple-element.244, s32[512]{0:T(512)S(1)} %fusion.67), kind=kCustom, calls=%fused_computation.clone.1 | custom fusion | bytes 528384 | tf_op jit(solution)/shard_map/while/body/jit(take_along_axis)/gather | solution.py:36
  273.2 4.8 %gather_fusion = f32[512]{0:T(512)S(1)} fusion(f32[4,1920]{1,0:T(4,128)S(1)} %get-tuple-element.251, s32[512]{0:T(512)S(1)} %fusion.67), kind=kCustom, calls=%fused_computation.1.clone.1 | custom fusion | bytes 8192 | tf_op jit(solution)/shard_map/while/body/jit(take_along_axis)/gather | solution.py:37
  279.6 6.6 %gather_fusion.1 = bf16[512,256]{1,0:T(8,128)(2,1)S(1)} fusion(bf16[4,256,1920]{1,2,0:T(8,128)(2,1)} %get-tuple-element.244, s32[512]{0:T(512)S(1)} %fusion.67), kind=kCustom, calls=%fused_computation.clone.1 | custom fusion | bytes 528384 | tf_op jit(solution)/shard_map/while/body/jit(take_along_axis)/gather | solution.py:36
  287.8 4.8 %gather_fusion = f32[512]{0:T(512)S(1)} fusion(f32[4,1920]{1,0:T(4,128)S(1)} %get-tuple-element.251, s32[512]{0:T(512)S(1)} %fusion.67), kind=kCustom, calls=%fused_computation.1.clone.1 | custom fusion | bytes 8192 | tf_op jit(solution)/shard_map/while/body/jit(take_along_axis)/gather | solution.py:37
  294.2 6.6 %gather_fusion.1 = bf16[512,256]{1,0:T(8,128)(2,1)S(1)} fusion(bf16[4,256,1920]{1,2,0:T(8,128)(2,1)} %get-tuple-element.244, s32[512]{0:T(512)S(1)} %fusion.67), kind=kCustom, calls=%fused_computation.clone.1 | custom fusion | bytes 528384 | tf_op jit(solution)/shard_map/while/body/jit(take_along_axis)/gather | solution.py:36
  302.4 4.8 %gather_fusion = f32[512]{0:T(512)S(1)} fusion(f32[4,1920]{1,0:T(4,128)S(1)} %get-tuple-element.251, s32[512]{0:T(512)S(1)} %fusion.67), kind=kCustom, calls=%fused_computation.1.clone.1 | custom fusion | bytes 8192 | tf_op jit(solution)/shard_map/while/body/jit(take_along_axis)/gather | solution.py:37
  308.8 6.7 %gather_fusion.1 = bf16[512,256]{1,0:T(8,128)(2,1)S(1)} fusion(bf16[4,256,1920]{1,2,0:T(8,128)(2,1)} %get-tuple-element.244, s32[512]{0:T(512)S(1)} %fusion.67), kind=kCustom, calls=%fused_computation.clone.1 | custom fusion | bytes 528384 | tf_op jit(solution)/shard_map/while/body/jit(take_along_axis)/gather | solution.py:36
  317.0 4.8 %gather_fusion = f32[512]{0:T(512)S(1)} fusion(f32[4,1920]{1,0:T(4,128)S(1)} %get-tuple-element.251, s32[512]{0:T(512)S(1)} %fusion.67), kind=kCustom, calls=%fused_computation.1.clone.1 | custom fusion | bytes 8192 | tf_op jit(solution)/shard_map/while/body/jit(take_along_axis)/gather | solution.py:37
  323.4 6.6 %gather_fusion.1 = bf16[512,256]{1,0:T(8,128)(2,1)S(1)} fusion(bf16[4,256,1920]{1,2,0:T(8,128)(2,1)} %get-tuple-element.244, s32[512]{0:T(512)S(1)} %fusion.67), kind=kCustom, calls=%fused_computation.clone.1 | custom fusion | bytes 528384 | tf_op jit(solution)/shard_map/while/body/jit(take_along_axis)/gather | solution.py:36
  331.6 4.8 %gather_fusion = f32[512]{0:T(512)S(1)} fusion(f32[4,1920]{1,0:T(4,128)S(1)} %get-tuple-element.251, s32[512]{0:T(512)S(1)} %fusion.67), kind=kCustom, calls=%fused_computation.1.clone.1 | custom fusion | bytes 8192 | tf_op jit(solution)/shard_map/while/body/jit(take_along_axis)/gather | solution.py:37
  338.0 6.6 %gather_fusion.1 = bf16[512,256]{1,0:T(8,128)(2,1)S(1)} fusion(bf16[4,256,1920]{1,2,0:T(8,128)(2,1)} %get-tuple-element.244, s32[512]{0:T(512)S(1)} %fusion.67), kind=kCustom, calls=%fused_computation.clone.1 | custom fusion | bytes 528384 | tf_op jit(solution)/shard_map/while/body/jit(take_along_axis)/gather | solution.py:36
  365.8 24.7 %all_to_all.37 = bf16[256,4,4,128]{3,2,1,0:T(4,128)(2,1)S(1)} all-to-all(bf16[256,4,4,128]{3,2,1,0:T(4,128)(2,1)S(1)} %copy.71), channel_id=1, replica_groups=mesh['mem'=32,'col'=8] {'mem'}, dimensions={0} | all-to-all | bytes 2097152 | tf_op jit(solution)/shard_map/all_to_all | solution.py:160
  (200 shorter events, 94.3 us)
Async XLA Ops:
  0.0 32.2 %copy-start.7 = (s32[1,4]{1,0:T(1,128)S(1)}, s32[1,4]{1,0:T(1,128)}, u32[]{:S(2)}) copy-start(s32[1,4]{1,0:T(1,128)} %param.10) | copy-start | bytes 52
  27.8 18.6 %copy-start.1 = (bf16[32,8,4,4,128]{4,1,0,3,2:T(8,128)(2,1)}, bf16[32,8,4,4,128]{4,1,0,3,2:T(8,128)(2,1)S(1)}, u32[]{:S(2)}) copy-start(bf16[32,8,4,4,128]{4,1,0,3,2:T(8,128)(2,1)S(1)} %copy.98) | copy-start | bytes 3145732
  27.8 14.2 %collective-permute-start = (bf16[256,4,4,128]{3,0,2,1:T(8,128)(2,1)S(1)}, bf16[256,4,4,128]{3,0,2,1:T(8,128)(2,1)S(1)}, u32[]{:S(2)}, u32[]{:S(2)}) collective-permute-start(bf16[256,4,4,128]{3,0,2,1:T(8,128)(2,1)S(1)} %bitcast.96), channel_id=1, source_target_pairs={{0,8},{8,16},{16,24},{24,32},{32,40},{40,48},{48,56},{56,64},{64,7... | collective-permute-start | bytes 3145736 | tf_op jit(solution)/shard_map/ppermute | solution.py:20
  30.3 16.1 %collective-permute-start.1 = (bf16[256,4,4,128]{3,0,2,1:T(8,128)(2,1)S(1)}, bf16[256,4,4,128]{3,0,2,1:T(8,128)(2,1)S(1)}, u32[]{:S(2)}, u32[]{:S(2)}) collective-permute-start(bf16[256,4,4,128]{3,0,2,1:T(8,128)(2,1)S(1)} %bitcast.97), channel_id=1, source_target_pairs={{8,0},{16,8},{24,16},{32,24},{40,32},{48,40},{56,48},{64,56},{72,6... | collective-permute-start | bytes 3145736 | tf_op jit(solution)/shard_map/ppermute | solution.py:23
  42.0 4.4 %copy-start.2 = (bf16[256,4,4,128]{3,0,2,1:T(8,128)(2,1)}, bf16[256,4,4,128]{3,0,2,1:T(8,128)(2,1)S(1)}, u32[]{:S(2)}) copy-start(bf16[256,4,4,128]{3,0,2,1:T(8,128)(2,1)S(1)} %collective-permute-done) | copy-start | bytes 3145732
  46.4 1.0 copy-start.3
  54.0 8.6 %collective-permute-start.2 = (bf16[256,4,12,4]{0,3,2,1:T(4,128)(2,1)S(1)}, bf16[256,4,12,4]{0,3,2,1:T(4,128)(2,1)}, u32[]{:S(2)}, u32[]{:S(2)}) collective-permute-start(bf16[256,4,12,4]{0,3,2,1:T(4,128)(2,1)S(1)} %copy.59), channel_id=1, source_target_pairs={{0,1},{1,2},{2,3},{3,4},{4,5},{5,6},{6,7},{8,9},{9,10},{10,11},{11... | collective-permute-start | bytes 294920 | tf_op jit(solution)/shard_map/ppermute | solution.py:20
  60.3 5.7 %collective-permute-start.3 = (bf16[256,4,12,4]{0,3,2,1:T(4,128)(2,1)}, bf16[256,4,12,4]{0,3,2,1:T(4,128)(2,1)}, u32[]{:S(2)}, u32[]{:S(2)}) collective-permute-start(bf16[256,4,12,4]{0,3,2,1:T(4,128)(2,1)} %copy.60), channel_id=1, source_target_pairs={{1,0},{2,1},{3,2},{4,3},{5,4},{6,5},{7,6},{9,8},{10,9},{11,10},{12... | collective-permute-start | bytes 294920 | tf_op jit(solution)/shard_map/ppermute | solution.py:23
  87.9 5.4 %copy-start = (bf16[256,4,12,136]{3,0,2,1:T(8,128)(2,1)}, bf16[256,4,12,136]{3,0,2,1:T(8,128)(2,1)S(1)}, u32[]{:S(2)}) copy-start(bf16[256,4,12,136]{3,0,2,1:T(8,128)(2,1)S(1)} %subtract_convert_fusion) | copy-start | bytes 10027012
  101.4 6.3 %copy-start.6 = (f32[1,1920]{1,0:T(1,128)S(1)}, f32[1,1920]{1,0:T(1,128)}, u32[]{:S(2)}) copy-start(f32[1,1920]{1,0:T(1,128)} %stack.37) | copy-start | bytes 23044
  107.8 3.8 copy-start.8
  107.8 3.8 copy-start.9
  111.6 234.2 %copy-start.4 = (f32[256,256]{1,0:T(8,128)S(1)}, f32[256,256]{1,0:T(8,128)}, u32[]{:S(2)}) copy-start(f32[256,256]{1,0:T(8,128)} %get-tuple-element.118) | copy-start | bytes 786436
  111.6 234.4 %copy-start.5 = (f32[256,256]{1,0:T(8,128)S(1)}, f32[256,256]{1,0:T(8,128)}, u32[]{:S(2)}) copy-start(f32[256,256]{1,0:T(8,128)} %fusion.22) | copy-start | bytes 786436
where the time goes:
time: 395 us; the launch traced here: 392 us
  local copies, waits for them, and re-layouts  243 us (62%)
  blocking collectives  50.3 us (13%)
  other arithmetic  39.9 us (10%)
  matrix products  33.8 us (9%)
  waiting for transfers between devices  13 us (3%)
  starting transfers between devices  10.1 us (3%)
    gather x32, local copies, waits for them, and re-layouts, observe(): observed = jnp.take_along_axis(anomaly_flat, cell_ids[:, None, :], axis=2)  108 us
    gather x16, local copies, waits for them, and re-layouts, observe(): innovation = values - jnp.take_along_axis(average_flat, cell_ids, axis=1)  77.3 us
    all_to_all x1, blocking collectives, local(): lax.all_to_all(background_trials, 'mem', split_axis=2, concat_axis=0, til...  25.6 us
    all_to_all x1, blocking collectives, local(): lax.all_to_all(analysed, 'mem', split_axis=0, concat_axis=2, tiled=True)  24.7 us
    slice x5, local copies, waits for them, and re-layouts, local(): deviation_matrix[:, :, :, sector_index * SECTOR_SPAN:sector_index * SECTO...  19.8 us
    sub x16, other arithmetic, observe(): innovation = values - jnp.take_along_axis(average_flat, cell_ids, axis=1)  12.5 us
    gather x16, other arithmetic, observe(): observed = jnp.take_along_axis(anomaly_flat, cell_ids[:, None, :], axis=2)  11.2 us
    dynamic_slice x16, local copies, waits for them, and re-layouts, take_block(): return lax.dynamic_slice_in_dim(source, block_start, obs_block, 1)  11 us
  transfers between devices with their start and end apart: 4, of which 3 were waited for; matrix products, arithmetic and copies ran while one was open for 2% of the time, Pallas kernels for 0%

commit v1 on v0

v1 whole, which is shorter than its diff:
```python
import functools

import jax
import jax.numpy as jnp
from jax import lax
from jax.experimental import pallas as pl
from jax.experimental.pallas import tpu as pltpu
from jax.sharding import PartitionSpec as P

MESH = pl.DeviceIdType.MESH
F32 = jnp.float32
BF16 = jnp.bfloat16
N = 32
inflation = 1.1
members = 256


def iota(shape, dim):
    return lax.broadcasted_iota(jnp.int32, shape, dim)


def dot(a, b):
    return lax.dot_general(a, b, (((1,), (0,)), ((), ())), preferred_element_type=F32)


def dot_nt(a, b):
    return lax.dot_general(a, b, (((1,), (1,)), ((), ())), preferred_element_type=F32)


def split2(a):
    hi = a.astype(BF16)
    return hi, (a - hi.astype(F32)).astype(BF16)


def split3(a):
    hi = a.astype(BF16)
    rest = a - hi.astype(F32)
    mid = rest.astype(BF16)
    return hi, mid, (rest - mid.astype(F32)).astype(BF16)


def dot3(a, b):
    (ah, al), (bh, bl) = a, b
    return dot(
        jnp.concatenate([ah, ah, al], axis=1), jnp.concatenate([bh, bl, bh], axis=0)
    )


def swap_matrix():
    row, col = iota((512, 512), 0), iota((512, 512), 1)
    swapped = (col // 128) * 32 + ((col % 128) // 32) * 128 + col % 32
    return (row == swapped).astype(F32).astype(BF16)


def place(m):
    return (m // 8) * 2 + m % 2, (m // 2) % 4


def device_of(g, b):
    return (g // 2) * 8 + b * 2 + g % 2


def histogram(me, z, counts, cells, classes, readings, inv_var, table, out_ref):
    e = cells[...]
    s = (e >= 480).astype(jnp.int32) + (e >= 960).astype(jnp.int32) + (e >= 1440).astype(jnp.int32)
    rest = e - s * 480
    r = (rest * 1639) // 65536
    c = rest - r * 40
    dt = r // 4
    left, right = c < 4, c >= 36
    side = left | right
    slab = dt * 5 + jnp.where(side, 4, s)
    lane = jnp.where(
        side,
        jnp.where(right, 64, 0) + s * 16 + (r % 4) * 4 + c % 4,
        (r % 4) * 32 + c - 4,
    )
    column = z * 4 + iota(e.shape, 0)
    outside = (
        ((dt == 0) & (me == 0))
        | ((dt == 2) & (me == N - 1))
        | (left & (column == 0))
        | (right & (column == 31))
    )
    kind = classes[...]
    factor = jnp.zeros(e.shape, F32)
    for i in range(16):
        factor = jnp.where(kind == i, table[i], factor)
    live = (iota(e.shape, 1) < counts[...]) & ~outside
    weight = jnp.where(live, inv_var[...] * factor, 0.0)
    product = weight * readings[...]
    w_parts, v_parts = split3(weight), split3(product)
    for b in range(4):
        lanes = (iota((128, 2048), 0) == lane[b : b + 1]).astype(F32).astype(BF16)
        here = iota((16, 2048), 0) == slab[b : b + 1]
        rows = [
            jnp.where(here, part[b : b + 1].astype(F32), 0.0).astype(BF16)
            for part in w_parts + v_parts
        ]
        sums = dot_nt(jnp.concatenate(rows, axis=0), lanes)
        out_ref[b, 0] = sums[0:16] + sums[16:32] + sums[32:48]
        out_ref[b, 1] = sums[48:64] + sums[64:80] + sums[80:96]


def spread_kernel(
    x_ref, counts, cells, classes, readings, inv_var, table,
    tiles_ref, sums_ref,
    packed, mine, edge, edge_in,
    send, recv, edge_send, edge_recv, sums_send, sums_recv, halo_send, halo_recv,
):
    me = lax.axis_index("mem")
    z = lax.axis_index("col")
    g, b_me = place(me)
    barrier = pltpu.get_barrier_semaphore()

    def greet(i, carry):
        pl.semaphore_signal(
            barrier, inc=1, device_id={"mem": lax.rem(me + i, N)}, device_id_type=MESH
        )
        return carry

    lax.fori_loop(1, N, greet, 0)
    z_sides = (lax.rem(z + 1, 8), lax.rem(z + 7, 8))
    for other in z_sides:
        pl.semaphore_signal(barrier, inc=1, device_id={"col": other}, device_id_type=MESH)
    pl.semaphore_wait(barrier, N + 1)

    row, col = iota((128, 128), 0), iota((128, 128), 1)
    edge_pick = row == jnp.where(col < 64, 124, 0) + col % 4
    edges = jnp.zeros((256, 128), F32)
    for sr in range(16):
        pick = (edge_pick & ((col // 4) % 16 == sr)).astype(F32).astype(BF16)
        edges = edges + dot(x_ref[sr], pick)
    edge[...] = edges.astype(BF16)
    edge_copies = []
    for k, other in enumerate(z_sides):
        copy = pltpu.make_async_remote_copy(
            src_ref=edge, dst_ref=edge_in.at[k], send_sem=edge_send.at[k],
            recv_sem=edge_recv.at[k], device_id={"col": other}, device_id_type=MESH,
        )
        copy.start()
        edge_copies.append(copy)

    def send_slab(s):
        rows = pl.ds(pl.multiple_of(me * 8, 8), 8)
        pltpu.make_async_copy(
            packed.at[s, b_me * 8 + g], tiles_ref.at[pl.ds(1, 4), s, rows], recv.at[s]
        ).start()

        def one(i, carry):
            to = lax.rem(me + i, N)
            g_to, b_to = place(to)
            pltpu.make_async_remote_copy(
                src_ref=packed.at[s, b_to * 8 + g_to],
                dst_ref=tiles_ref.at[pl.ds(1, 4), s, rows],
                send_sem=send.at[s], recv_sem=recv.at[s],
                device_id={"mem": to}, device_id_type=MESH,
            ).start()
            return carry

        lax.fori_loop(1, N, one, 0)

    swap = swap_matrix()
    for s in range(4):
        wide = jnp.concatenate([x_ref[4 * s + r] for r in range(4)], axis=1)
        out = dot(wide, swap).astype(BF16)
        for b in range(4):
            packed[s, 8 * b : 8 * b + 8] = out[:, 128 * b : 128 * b + 128].reshape(8, 4, 8, 128)
        send_slab(s)

    row, col = iota((128, 512), 0), iota((128, 512), 1)
    side_pick = row == (col // 128) * 32 + jnp.where(col % 128 < 64, -4, 32) + col % 4
    sides = jnp.zeros((256, 512), F32)
    for sr in range(16):
        pick = (side_pick & ((col // 4) % 16 == sr)).astype(F32).astype(BF16)
        sides = sides + dot(x_ref[sr], pick)
    for copy in edge_copies:
        copy.wait()
    lane = iota((256, 128), 1)
    for b in range(4):
        part = sides[:, 128 * b : 128 * b + 128]
        if b == 0:
            part = part + jnp.where(lane < 64, edge_in[0].astype(F32), 0.0)
        if b == 3:
            part = part + jnp.where(lane < 64, 0.0, edge_in[1].astype(F32))
        packed[4, 8 * b : 8 * b + 8] = part.astype(BF16).reshape(8, 4, 8, 128)
    send_slab(4)

    histogram(me, z, counts, cells, classes, readings, inv_var, table, mine)
    for b in range(4):
        to = device_of(me // 4, b)

        def sums_copy():
            return pltpu.make_async_remote_copy(
                src_ref=mine.at[b], dst_ref=sums_ref.at[lax.rem(me, 4)],
                send_sem=sums_send.at[b], recv_sem=sums_recv,
                device_id={"mem": to}, device_id_type=MESH,
            )

        @pl.when(to != me)
        def _():
            sums_copy().start()

        @pl.when(to == me)
        def _():
            pltpu.make_async_copy(mine.at[b], sums_ref.at[lax.rem(me, 4)], sums_recv).start()

    for s in range(5):
        whole = tiles_ref.at[pl.ds(1, 4), s]
        pltpu.make_async_copy(whole, whole, recv.at[s]).wait()

    down = device_of(lax.rem(g + 1, 8), b_me)
    up = device_of(lax.rem(g + 7, 8), b_me)
    halo_copies = []
    for k, (to, mine_at, theirs_at) in enumerate(((down, 4, 0), (up, 1, 5))):
        copy = pltpu.make_async_remote_copy(
            src_ref=tiles_ref.at[mine_at], dst_ref=tiles_ref.at[theirs_at],
            send_sem=halo_send.at[k], recv_sem=halo_recv.at[k],
            device_id={"mem": to}, device_id_type=MESH,
        )
        copy.start()
        halo_copies.append(copy)
    for s in range(5):
        some = packed.at[s, pl.ds(0, N - 1)]
        pltpu.make_async_copy(some, some, send.at[s]).wait()
    for b in range(4):
        to = device_of(me // 4, b)

        @pl.when(to != me)
        def _():
            pltpu.make_async_copy(mine.at[b], mine.at[b], sums_send.at[b]).wait()

    pltpu.make_async_copy(sums_ref, sums_ref, sums_recv).wait()
    for copy in halo_copies:
        copy.wait()


def analyse_kernel(tiles_ref, sums_ref, out_ref, anomaly, average):
    for t in range(6):
        for s in range(5):
            x = tiles_ref[t, s].astype(F32)
            mean = jnp.sum(x, axis=0, keepdims=True) * (1.0 / members)
            average[t, s : s + 1] = mean
            anomaly[t, s] = (x - mean).astype(BF16)
    diagonal = iota((256, 256), 0) == iota((256, 256), 1)
    eye = jnp.where(diagonal, 1.0, 0.0)
    for p in range(4):
        gram = (members - 1) / inflation * eye
        force = jnp.zeros((16, 256), F32)
        for dt in range(3):
            scaled, plain = [], []
            means = average[p + dt]
            weights = sums_ref[p, 0, 5 * dt : 5 * dt + 5]
            products = sums_ref[p, 1, 5 * dt : 5 * dt + 5]
            shift = split3(products - means[0:5] * weights)
            for s in range(5):
                a = anomaly[p + dt, s]
                plain.append(a)
                body = (a.astype(F32) * weights[s : s + 1]).astype(BF16)
                extra = jnp.concatenate(
                    [part[s : s + 1].astype(F32) for part in shift] + [jnp.zeros((13, 128), F32)],
                    axis=0,
                ).astype(BF16)
                scaled.append(jnp.concatenate([body, extra], axis=0))
            both = dot_nt(jnp.concatenate(scaled, axis=1), jnp.concatenate(plain, axis=1))
            gram = gram + both[0:256]
            force = force + both[256:272]
        forcing = jnp.sum(force, axis=0, keepdims=True)
        norm = jnp.sqrt(jnp.sum(jnp.sum(gram * gram, axis=0, keepdims=True), axis=1, keepdims=True))
        y = gram / norm
        y0s = split2(y)
        y1 = 1.5 * y - 0.5 * dot3(y0s, y0s)
        z1 = 1.5 * eye - 0.5 * y
        y1s = split2(y1)
        q = 1.5 * y1 - 0.5 * dot3(y0s, y1s)
        qs = split2(q)
        y2 = 1.5 * y1 - 0.5 * dot3(y1s, qs)
        z2 = 1.5 * z1 - 0.5 * dot3(qs, split2(z1))
        y2s, z2s = split2(y2), split2(z2)
        qs = split2(dot3(z2s, y2s))
        y3 = 1.5 * y2 - 0.5 * dot3(y2s, qs)
        z3 = 1.5 * z2 - 0.5 * dot3(qs, z2s)
        z3s = split2(z3)
        qs = split2(dot3(z3s, split2(y3)))
        root = 1.5 * z3 - 0.5 * dot3(qs, z3s)
        rh, rl = split2(root)

        def times_root(v):
            parts = jnp.concatenate(
                [part.astype(F32) for part in split3(v)] + [jnp.zeros((13, 256), F32)], axis=0
            ).astype(BF16)
            return jnp.sum(dot(parts, rh) + dot(parts, rl), axis=0, keepdims=True)

        mean_shift = times_root(times_root(forcing)) / norm
        transform = (jnp.sqrt((members - 1.0) / norm) * root + mean_shift).astype(BF16)
        for s in range(4):
            out = dot(transform, anomaly[p + 1, s]) + average[p + 1, s : s + 1]
            out_ref[s, p] = out.astype(BF16)


def collect_kernel(a_ref, out_ref, got, send, recv):
    me = lax.axis_index("mem")
    g, b_me = place(me)
    barrier = pltpu.get_barrier_semaphore()

    def greet(i, carry):
        pl.semaphore_signal(
            barrier, inc=1, device_id={"mem": lax.rem(me + i, N)}, device_id_type=MESH
        )
        return carry

    lax.fori_loop(1, N, greet, 0)
    pl.semaphore_wait(barrier, N - 1)

    def rows(m):
        return pl.ds(pl.multiple_of(m * 8, 8), 8)

    place_at = got.at[:, b_me, pl.ds(g * 4, 4)]
    pltpu.make_async_copy(a_ref.at[:, :, rows(me)], place_at, recv).start()

    def one(i, carry):
        to = lax.rem(me + i, N)
        pltpu.make_async_remote_copy(
            src_ref=a_ref.at[:, :, rows(to)], dst_ref=place_at,
            send_sem=send, recv_sem=recv, device_id={"mem": to}, device_id_type=MESH,
        ).start()
        return carry

    lax.fori_loop(1, N, one, 0)
    swap = swap_matrix()
    pltpu.make_async_copy(got, got, recv).wait()
    for s in range(4):
        wide = jnp.concatenate([got[s, b].reshape(256, 128) for b in range(4)], axis=1)
        out = dot(wide, swap).astype(BF16)
        for r in range(4):
            out_ref[s, r] = out[:, 128 * r : 128 * r + 128]
    some = a_ref.at[:, :, pl.ds(0, 248)]
    pltpu.make_async_copy(some, some, send).wait()


def vmem():
    return pl.BlockSpec(memory_space=pltpu.VMEM)


def params(collective_id=None):
    extra = {} if collective_id is None else {"collective_id": collective_id, "has_side_effects": True}
    return pltpu.CompilerParams(vmem_limit_bytes=48 << 20, **extra)


def local(trials, tally, cells, classes, readings, inv_var, table):
    x = trials.reshape(8, 4, 32, 4, 128).transpose(1, 3, 2, 0, 4).reshape(16, 256, 128)
    dma = pltpu.SemaphoreType.DMA
    tiles, sums = pl.pallas_call(
        spread_kernel,
        out_shape=[
            jax.ShapeDtypeStruct((6, 5, 256, 128), BF16),
            jax.ShapeDtypeStruct((4, 2, 16, 128), F32),
        ],
        in_specs=[vmem()] * 6 + [pl.BlockSpec(memory_space=pltpu.SMEM)],
        out_specs=[vmem()] * 2,
        scratch_shapes=[
            pltpu.VMEM((5, 32, 4, 8, 128), BF16),
            pltpu.VMEM((4, 2, 16, 128), F32),
            pltpu.VMEM((256, 128), BF16),
            pltpu.VMEM((2, 256, 128), BF16),
            dma((5,)), dma((5,)), dma((2,)), dma((2,)), dma((4,)), dma, dma((2,)), dma((2,)),
        ],
        compiler_params=params(0),
        name="spread",
    )(
        x,
        tally.reshape(4, 1),
        cells.reshape(4, 2048),
        classes.reshape(4, 2048),
        readings.reshape(4, 2048),
        inv_var.reshape(4, 2048),
        table,
    )
    analysed = pl.pallas_call(
        analyse_kernel,
        out_shape=jax.ShapeDtypeStruct((4, 4, 256, 128), BF16),
        in_specs=[vmem()] * 2,
        out_specs=vmem(),
        scratch_shapes=[pltpu.VMEM((6, 5, 256, 128), BF16), pltpu.VMEM((6, 8, 128), F32)],
        compiler_params=params(),
        name="analyse",
    )(tiles, sums)
    out = pl.pallas_call(
        collect_kernel,
        out_shape=jax.ShapeDtypeStruct((4, 4, 256, 128), BF16),
        in_specs=[vmem()],
        out_specs=vmem(),
        scratch_shapes=[pltpu.VMEM((4, 4, 32, 8, 128), BF16), dma, dma],
        compiler_params=params(1),
        name="collect",
    )(analysed)
    return out.reshape(4, 4, 32, 8, 128).transpose(3, 0, 2, 1, 4).reshape(8, 4, 128, 128)


def solution(mesh):
    placed = (
        P("mem", None, None, "col"),
        P("mem", "col"),
        P("mem", "col", None),
        P("mem", "col", None),
        P("mem", "col", None),
        P("mem", "col", None),
        P(),
    )
    return jax.shard_map(
        local, mesh=mesh, in_specs=placed, out_specs=P("mem", None, None, "col"), check_vma=False
    )
```

time: 395 us -> 74.4 us (0.19)
  local copies, waits for them, and re-layouts: 243 us -> 4.5 us
  Pallas kernels: 0 us -> 69.7 us
  blocking collectives: 50.3 us -> 0 us
  other arithmetic: 39.9 us -> 0 us
  matrix products: 33.8 us -> 0 us
  waiting for transfers between devices: 13 us -> 0 us
  starting transfers between devices: 10.1 us -> 0 us
    gather x48 -> x0, local copies, waits for them, and re-layouts: 186 us -> none  [the longest x32 108 us: observe(): observed = jnp.take_along_axis(anomaly_flat, cell_ids[:, None, :], axis=2)]
    pallas_call x0 -> x3, Pallas kernels: none -> 69.7 us  [the longest x1 34.7 us: local(): pl.pallas_call(spread_kernel, out_shape=[jax.ShapeDtypeStruct((6, 5, 256,...]
    all_to_all x2 -> x0, blocking collectives: 50.3 us -> none  [the longest x1 25.6 us: local(): lax.all_to_all(background_trials, 'mem', split_axis=2, concat_axis=0, til...]
    dot_general x47 -> x0, matrix products: 33.8 us -> none  [the longest x1 7.08 us: local(): lax.dot_general(unit_weights, enlarged_piece, (((0,), (0,)), ((), ())), p...]
    slice x12 -> x0, local copies, waits for them, and re-layouts: 31.5 us -> none  [the longest x5 19.8 us: local(): deviation_matrix[:, :, :, sector_index * SECTOR_SPAN:sector_index * SECTO...]
    ppermute x4 -> x0, waiting for transfers between devices: 13 us -> none  [the longest x2 7.75 us: padded(): lax.ppermute(lax.slice_in_dim(block, block.shape[dim] - width, None, axis...]
    sub x16 -> x0, other arithmetic: 12.5 us -> none  [observe(): innovation = values - jnp.take_along_axis(average_flat, cell_ids, axis=1)]
    gather x16 -> x0, other arithmetic: 11.2 us -> none  [observe(): observed = jnp.take_along_axis(anomaly_flat, cell_ids[:, None, :], axis=2)]
  transfers between devices with their start and end apart: 4 -> 0, of which waited for: 3 -> 0; matrix products, arithmetic and copies ran while one was open for 2% -> 0% of each run, Pallas kernels for 0% -> 0%
where the time goes in v1:
time: 74.4 us; the launch traced here: 74.2 us
  Pallas kernels  69.7 us (94%)
  local copies, waits for them, and re-layouts  4.5 us (6%)
    pallas_call x1, Pallas kernels, local(): pl.pallas_call(spread_kernel, out_shape=[jax.ShapeDtypeStruct((6, 5, 256,...  34.7 us
    pallas_call x1, Pallas kernels, local(): pl.pallas_call(collect_kernel, out_shape=jax.ShapeDtypeStruct((4, 4, 256,...  19.9 us
    pallas_call x1, Pallas kernels, local(): pl.pallas_call(analyse_kernel, out_shape=jax.ShapeDtypeStruct((4, 4, 256,...  15.1 us
    reshape x1, local copies, waits for them, and re-layouts, local(): trials.reshape(8, 4, 32, 4, 128).transpose(1, 3, 2, 0, 4)  1.9 us
    transpose x1, local copies, waits for them, and re-layouts, local(): out.reshape(4, 4, 32, 8, 128).transpose(3, 0, 2, 1, 4)  1.78 us

profile of v1, /device:TPU:1, one launch (start us, length us, event | category | flops | bytes accessed | tf_op | source)
XLA Modules:
  0.0 74.2 jit_solution(10777492306878849139)
XLA Ops:
  0.0 0.0 copy-start.4
  0.0 0.0 copy-start.3
  0.0 0.0 copy-start.2
  0.0 0.0 copy-start.1
  0.0 0.0 copy-start
  0.0 0.8 %copy.9.counts = s32[4,1]{1,0:T(4,128)S(1)} copy(s32[4,1]{0,1:T(1,128)} %bitcast.20) | data formatting | bytes 32 | tf_op jit(solution)/shard_map/reshape | solution.py:372
  0.8 1.9 %copy.8 = bf16[8,4,32,4,128]{4,0,2,3,1:T(8,128)(2,1)S(1)} copy(bf16[8,4,32,4,128]{4,3,2,1,0:T(4,128)(2,1)} %bitcast.19) | data formatting | bytes 2097152 | tf_op jit(solution)/shard_map/reshape | solution.py:351
  2.7 0.0 copy-done.4
  2.7 0.0 copy-done.3
  2.8 0.0 copy-done.2
  2.8 0.0 copy-done.1
  2.8 0.0 copy-done
  2.8 34.7 %spread.1 = (bf16[6,5,256,128]{3,2,1,0:T(8,128)(2,1)S(1)}, f32[4,2,16,128]{3,2,1,0:T(8,128)S(1)}) custom-call(bf16[16,256,128]{2,1,0:T(8,128)(2,1)S(1)} %bitcast.13, s32[4,1]{1,0:T(4,128)S(1)} %copy.9.counts, s32[4,2048]{1,0:T(4,128)S(1)} %bitcast.15, s32[4,2048]{1,0:T(4,128)S(1)} %bitcast.16, f32[4,2048]{1,0:T(4,128)S(1)} %bitcast.17, ...), custom_call_target="tpu_custom_call" | custom-call | tf_op jit(solution)/shard_map/spread/pallas_call | solution.py:353
  37.5 15.1 %analyse.1.a_ref = bf16[4,4,256,128]{3,2,1,0:T(8,128)(2,1)S(1)} custom-call(bf16[6,5,256,128]{3,2,1,0:T(8,128)(2,1)S(1)} %get-tuple-element.7.tiles_ref, f32[4,2,16,128]{3,2,1,0:T(8,128)S(1)} %get-tuple-element.8.sums_ref), custom_call_target="tpu_custom_call" | custom-call | tf_op jit(solution)/shard_map/analyse/pallas_call | solution.py:379
  52.6 19.9 %collect.1 = bf16[4,4,256,128]{3,2,1,0:T(8,128)(2,1)S(1)} custom-call(bf16[4,4,256,128]{3,2,1,0:T(8,128)(2,1)S(1)} %analyse.1.a_ref), custom_call_target="tpu_custom_call" | custom-call | tf_op jit(solution)/shard_map/collect/pallas_call | solution.py:388
  72.5 1.8 %copy.10 = bf16[8,4,32,4,128]{4,3,2,1,0:T(4,128)(2,1)} copy(bf16[8,4,32,4,128]{4,0,2,3,1:T(8,128)(2,1)S(1)} %bitcast.14) | data formatting | bytes 2097152 | tf_op jit(solution)/shard_map/transpose | solution.py:397
Async XLA Ops:
  0.0 2.7 %copy-start.4 = (f32[16]{0:T(128)S(1)}, f32[16]{0:T(128)}, u32[]{:S(2)}) copy-start(f32[16]{0:T(128)} %table.1) | copy-start | bytes 196
  0.0 2.7 %copy-start.3 = (f32[1,4,2048]{2,1,0:T(4,128)S(1)}, f32[1,4,2048]{2,1,0:T(4,128)}, u32[]{:S(2)}) copy-start(f32[1,4,2048]{2,1,0:T(4,128)} %param.12) | copy-start | bytes 98308
  0.0 2.7 %copy-start.2 = (f32[1,4,2048]{2,1,0:T(4,128)S(1)}, f32[1,4,2048]{2,1,0:T(4,128)}, u32[]{:S(2)}) copy-start(f32[1,4,2048]{2,1,0:T(4,128)} %param.11) | copy-start | bytes 98308
  0.0 2.8 %copy-start.1 = (s32[1,4,2048]{2,1,0:T(4,128)S(1)}, s32[1,4,2048]{2,1,0:T(4,128)}, u32[]{:S(2)}) copy-start(s32[1,4,2048]{2,1,0:T(4,128)} %param.10) | copy-start | bytes 98308
  0.0 2.8 %copy-start = (s32[1,4,2048]{2,1,0:T(4,128)S(1)}, s32[1,4,2048]{2,1,0:T(4,128)}, u32[]{:S(2)}) copy-start(s32[1,4,2048]{2,1,0:T(4,128)} %param.9) | copy-start | bytes 98308
